TPU v7x, 256 devices: a whole 4x4x8 slice. The times are simulated.
256 devices in a mesh: wide: 32 (over y_lo, z, core), narrow: 8 (over x, y_hi).
Axes of the slice: x: 4, y: 4 (y_hi: 2, y_lo: 2; y = y_hi * 2 + y_lo), z: 8, core: 2. Of those that a mesh axis runs over, the one named last changes fastest.
Arguments:
- dark: bfloat16 [64, 32, 8, 16], P(None, None, 'narrow'), may hold values from -6 to 6
- w_enc: bfloat16 [27, 64, 64], replicated, may hold values from -0.15625 to 0.15625
- up_weight: bfloat16 [512, 16, 64], replicated, may hold values from -0.75 to 0.75
- w_dec: bfloat16 [27, 16, 16], replicated, may hold values from -0.3125 to 0.3125
- cotangent: bfloat16 [16, 256, 64, 128], P(None, 'wide', 'narrow'), may hold values from -6 to 6
Outputs:
- grad_dark: float32 [64, 32, 8, 16], P(None, None, 'narrow')
- grad_w_enc: float32 [27, 64, 64], replicated
- grad_up_weight: float32 [512, 16, 64], P(('wide', 'narrow'))
- grad_w_dec: float32 [27, 16, 16], replicated
All inputs are finite; a program needn't handle non-finite values.
Results may differ from a plain program's by a relative error of at most 0.0053.
Values may be sent and summed in bfloat16 or wider, within the bound.
A program may use at most 64 MiB of HBM per device.

v0:
```python
import math
import jax
import jax.numpy as jnp
from jax import lax
from jax.sharding import PartitionSpec as P

RATIO = 8


def padded_2(block, sides, width):
    for axis, dim in sides:
        count = lax.axis_size(axis)
        forward = [(i, i + 1) for i in range(count - 1)]
        backward = [(target, source) for source, target in forward]
        low = lax.ppermute(
            lax.slice_in_dim(block, block.shape[dim] - width, None, axis=dim), axis, forward
        )
        high = lax.ppermute(lax.slice_in_dim(block, 0, width, axis=dim), axis, backward)
        block = jnp.concatenate([low, block, high], axis=dim)
    return block


def silu_slope(values):
    sigma = jax.nn.sigmoid(values)
    return sigma * (1.0 + values * (1.0 - sigma))


def coarse_margin(field):
    return padded_2(field, (("narrow", 2),), 1)


def pad_coarse(field):
    return jnp.pad(field, ((0, 0), (1, 1), (0, 0), (1, 1)))


def pad_fine(field):
    return jnp.pad(field, ((0, 0), (0, 0), (0, 0), (1, 1)))


def flatten(kernel):
    return kernel.transpose(1, 0, 2).reshape(kernel.shape[1], -1)


def transposed(kernel):
    return kernel[::-1].transpose(2, 0, 1).reshape(kernel.shape[2], -1)


def unflatten(flat):
    return flat.reshape(flat.shape[0], 27, -1).transpose(1, 0, 2)


def columns(padded, first, count, depth, width):
    pieces = []
    for shift_x in range(3):
        for shift_z in range(3):
            for shift_y in range(3):
                pieces.append(
                    padded[
                        :,
                        first + shift_x : first + shift_x + count,
                        shift_z : shift_z + depth,
                        shift_y : shift_y + width,
                    ]
                )
    return jnp.concatenate(pieces, 0)


def block_size(planes):
    return planes // 4


def convolve_blocks(padded, flat):
    planes = padded.shape[1] - 2
    depth = padded.shape[2] - 2
    width = padded.shape[3] - 2
    block = block_size(planes)
    results = []
    for first in range(0, planes, block):
        stacked = columns(padded, first, block, depth, width)
        results.append(
            jnp.einsum("ok,kxzy->oxzy", flat, stacked, preferred_element_type=jnp.float32)
        )
    return jnp.concatenate(results, 1)


def upsample(table, enc_planes, ratio, fine_ch):
    chans = enc_planes.shape[0]
    planes = enc_planes.shape[1]
    depth = enc_planes.shape[2]
    width = enc_planes.shape[3]
    up_rows = jnp.dot(
        table, enc_planes.reshape(chans, planes * depth * width), preferred_element_type=jnp.float32
    )
    return (
        up_rows.reshape(ratio, ratio, ratio, fine_ch, planes, depth, width)
        .transpose(3, 4, 0, 5, 1, 6, 2)
        .reshape(fine_ch, planes * ratio, depth * ratio, width * ratio)
        .astype(jnp.bfloat16)
    )


def on_device(dark, w_enc, up_weight, w_dec, cotangent):
    ratio = RATIO
    chans = dark.shape[0]
    fine_ch = w_dec.shape[1]
    subs = up_weight.shape[0]
    wide_count = lax.axis_size("wide")
    narrow_count = lax.axis_size("narrow")
    coarse_planes = dark.shape[1]
    own_planes = coarse_planes // wide_count
    depth = dark.shape[2]
    width = dark.shape[3]
    first_plane = lax.axis_index("wide") * own_planes
    dark_padded = pad_coarse(coarse_margin(dark))
    enc_flat_kernel = flatten(w_enc)
    enc_pre = convolve_blocks(dark_padded, enc_flat_kernel)
    encoded = jax.nn.silu(enc_pre).astype(jnp.bfloat16)
    enc_window = lax.dynamic_slice_in_dim(
        jnp.pad(encoded, ((0, 0), (1, 1), (0, 0), (0, 0))), first_plane, own_planes + 2, 1
    )
    enc_own = enc_window[:, 1 : own_planes + 1]
    cells = own_planes * depth * width
    enc_flat = enc_own.reshape(chans, cells)
    table = up_weight.reshape(subs * fine_ch, chans)
    fine_planes = own_planes * ratio
    fine_depth = depth * ratio
    fine_width = width * ratio
    upsampled = upsample(table, enc_own, ratio, fine_ch)
    up_padded = pad_fine(padded_2(upsampled, (("wide", 1), ("narrow", 2)), 1))
    dec_flat = flatten(w_dec)
    cot_float = cotangent.astype(jnp.float32)
    block = block_size(fine_planes)
    grad_pieces = []
    dec_total = jnp.zeros((fine_ch, 27 * fine_ch), jnp.float32)
    for first in range(0, fine_planes, block):
        stacked = columns(up_padded, first, block, fine_depth, fine_width)
        pre_block = jnp.einsum(
            "ok,kxzy->oxzy", dec_flat, stacked, preferred_element_type=jnp.float32
        )
        piece = (cot_float[:, first : first + block] * silu_slope(pre_block)).astype(jnp.bfloat16)
        dec_total = dec_total + jnp.einsum(
            "oxzy,kxzy->ok", piece, stacked, preferred_element_type=jnp.float32
        )
        grad_pieces.append(piece)
    dec_grad = jnp.concatenate(grad_pieces, 1)
    grad_padded = pad_fine(padded_2(dec_grad, (("wide", 1), ("narrow", 2)), 1))
    back_up = convolve_blocks(grad_padded, transposed(w_dec))
    up_grad = (cot_float + back_up).astype(jnp.bfloat16)
    grad_rows = (
        up_grad.reshape(fine_ch, own_planes, ratio, depth, ratio, width, ratio)
        .transpose(2, 4, 6, 0, 1, 3, 5)
        .reshape(subs * fine_ch, cells)
    )
    enc_grad_own = (
        jnp.einsum("kc,kn->cn", table, grad_rows, preferred_element_type=jnp.float32)
        .reshape(chans, own_planes, depth, width)
        .astype(jnp.bfloat16)
    )
    enc_grad = lax.all_gather(enc_grad_own, "wide", axis=1, tiled=True)
    enc_pre_grad = (enc_grad.astype(jnp.float32) * silu_slope(enc_pre)).astype(jnp.bfloat16)
    grad_own = lax.dynamic_slice_in_dim(enc_pre_grad, first_plane, own_planes, 1)
    dark_own = lax.dynamic_slice_in_dim(dark_padded, first_plane, own_planes + 2, 1)
    stacked_own = columns(dark_own, 0, own_planes, depth, width)
    enc_total = jnp.einsum(
        "oxzy,kxzy->ok", grad_own, stacked_own, preferred_element_type=jnp.float32
    )
    grad_dark = convolve_blocks(pad_coarse(coarse_margin(enc_pre_grad)), transposed(w_enc))
    coarse_count = coarse_planes * depth * narrow_count * width
    coarse_scale = 1.0 / math.sqrt(coarse_count)
    fine_scale = 1.0 / math.sqrt(coarse_count * subs)
    owners = wide_count * narrow_count
    own_rows = subs // owners
    enc_sum, dec_sum, up_sum = lax.psum(
        (
            enc_total,
            dec_total,
            jnp.einsum(
                "kn,cn->kc", grad_rows, enc_flat, preferred_element_type=jnp.float32
            ).reshape(subs, fine_ch, chans),
        ),
        ("wide", "narrow"),
    )
    up_own = lax.dynamic_slice_in_dim(
        up_sum, lax.axis_index(("wide", "narrow")) * own_rows, own_rows, 0
    )
    return (
        grad_dark,
        unflatten(enc_sum) * coarse_scale,
        up_own * coarse_scale,
        unflatten(dec_sum) * fine_scale,
    )


def solution(mesh):
    in_specs = (P(None, None, "narrow", None), P(), P(), P(), P(None, "wide", "narrow", None))
    out_specs = (P(None, None, "narrow", None), P(), P(("wide", "narrow"), None, None), P())
    return jax.shard_map(
        on_device, mesh=mesh, in_specs=in_specs, out_specs=out_specs, check_vma=False
    )
```

profile of v0, /device:TPU:2, one launch (start us, length us, event | category | flops | bytes accessed | tf_op | source)
XLA Modules:
  0.0 539.2 jit_solution(12176044866597356027)
XLA Ops:
  7.2 5.1 collective-permute-start
  12.3 3.1 collective-permute-start.1
  15.5 1.6 fusion.88
  17.1 1.3 copy.39
  18.8 3.0 copy.48
  22.5 1.2 fusion.27
  27.7 1.7 fusion.87
  30.1 2.0 concatenate.180
  32.1 1.3 convolution_bitcast_fusion.15
  33.5 2.0 concatenate.182
  35.5 1.3 convolution_bitcast_fusion.14
  36.8 2.0 concatenate.184
  38.9 1.3 convolution_bitcast_fusion.13
  40.2 2.0 concatenate.186
  42.1 1.3 convolution_bitcast_fusion.12
  44.7 2.7 convert_element_type.71
  47.4 3.5 copy.96
  50.9 1.9 copy.50
  53.5 1.9 collective-permute-start.2
  55.4 1.3 collective-permute-start.3
  58.7 1.5 rev.6
  60.2 1.7 copy.56
  61.9 1.7 reshape.355
  63.6 1.7 copy.63
  66.3 1.3 pad_maximum_fusion.13
  67.7 4.2 collective-permute-start.4
  71.9 4.0 collective-permute-start.5
  76.7 1.5 concatenate.219
  78.2 1.4 collective-permute-done.5
  79.6 1.3 fusion.17
  85.5 3.3 collective-permute-start.6
  93.9 1.3 collective-permute-start.7
  95.3 83.9 %psum.23 = f32[16,432]{1,0:T(8,128)S(1)} all-reduce(f32[16,432]{1,0:T(8,128)S(1)} %fusion.7), channel_id=1, replica_groups=mesh['wide'=32,'narrow'=8] {'wide','narrow'}, use_global_device_ids=true, to_apply=%region_2.3 | all-reduce | flops 6912 | bytes 55296 | tf_op jit(solution)/shard_map/psum | solution.py:173
  179.8 3.6 collective-permute-start.8
  183.4 4.6 collective-permute-start.9
  198.5 1.8 copy.64
  200.2 4.1 copy.70
  204.3 3.5 copy.65
  207.9 4.7 reshape.344
  213.0 33.9 %all-gather = bf16[64,512]{0,1:T(8,128)(2,1)S(1)} all-gather(bf16[64,16]{0,1:T(8,128)(2,1)S(1)} %fusion.10), channel_id=2, replica_groups=mesh['wide'=32,'narrow'=8] {'wide'}, dimensions={1}, use_global_device_ids=true | all-gather | bytes 67584 | tf_op jit(solution)/shard_map/all_gather | solution.py:159
  247.0 5.8 %collective-permute-start.10 = (bf16[64,32,1,16]{0,3,1,2:T(8,128)(2,1)S(1)}, bf16[64,32,1,16]{0,3,1,2:T(8,128)(2,1)S(1)}, u32[]{:S(2)}, u32[]{:S(2)}) collective-permute-start(bf16[64,32,1,16]{0,3,1,2:T(8,128)(2,1)S(1)} %fusion.37), channel_id=1, source_target_pairs={{0,1},{1,2},{2,3},{3,4},{4,5},{5,6},{6,7},{8,9},{9,10},{10,11},{11... | collective-permute-start | bytes 196616 | tf_op jit(solution)/shard_map/ppermute | solution.py:15
  252.9 2.6 collective-permute-start.11
  255.6 2.8 fusion.1
  259.5 2.3 collective-permute-done.11
  265.1 1.3 concatenate.214
  266.4 1.3 concatenate.215
  271.7 256.2 %all-reduce.8.cloned.1.call-done = (f32[64,1728]{1,0:T(8,128)}, f32[512,16,64]{2,0,1:T(8,128)}) async-done(((f32[64,1728]{1,0:T(8,128)}, f32[512,16,64]{2,0,1:T(8,128)}), (f32[64,1728]{1,0:T(8,128)}, f32[512,16,64]{2,0,1:T(8,128)})) %all-reduce.8.cloned.1.call-update) | async-done | bytes 2539536 | tf_op jit(solution)/shard_map/psum | solution.py:173
  529.4 1.4 copy.73
  (280 shorter events, 43.3 us)
Async XLA Ops:
  7.2 520.8 %all-reduce.8.cloned.1.call-start = ((), (), s32[]{:S(2)}) async-start(), calls=%async_computation | async-start | bytes 9306112 | tf_op jit(solution)/shard_map/psum | solution.py:173
  7.2 14.7 %collective-permute-start = (bf16[64,32,1,16]{0,3,1,2:T(8,128)(2,1)}, bf16[64,32,1,16]{0,3,1,2:T(8,128)(2,1)S(1)}, u32[]{:S(2)}, u32[]{:S(2)}) collective-permute-start(bf16[64,32,1,16]{0,3,1,2:T(8,128)(2,1)} %bitcast.228), channel_id=1, source_target_pairs={{0,1},{1,2},{2,3},{3,4},{4,5},{5,6},{6,7},{8,9},{9,10},{10,11},{11... | collective-permute-start | bytes 196616 | tf_op jit(solution)/shard_map/ppermute | solution.py:15
  12.3 10.2 %collective-permute-start.1 = (bf16[64,32,1,16]{0,3,1,2:T(8,128)(2,1)}, bf16[64,32,1,16]{0,3,1,2:T(8,128)(2,1)}, u32[]{:S(2)}, u32[]{:S(2)}) collective-permute-start(bf16[64,32,1,16]{0,3,1,2:T(8,128)(2,1)} %bitcast.229), channel_id=1, source_target_pairs={{1,0},{2,1},{3,2},{4,3},{5,4},{6,5},{7,6},{9,8},{10,9},{11,10},{12... | collective-permute-start | bytes 196616 | tf_op jit(solution)/shard_map/ppermute | solution.py:18
  18.8 3.7 copy-start.2
  21.9 0.7 copy-start.3
  25.3 4.0 copy-start.4
  27.7 5.8 %copy-start.24 = (bf16[64,8,1,16]{0,3,1,2:T(8,128)(2,1)S(1)}, bf16[64,8,1,16]{0,3,1,2:T(8,128)(2,1)}, u32[]{:S(2)}) copy-start(bf16[64,8,1,16]{0,3,1,2:T(8,128)(2,1)} %get-tuple-element.345) | copy-start | bytes 49156
  27.7 5.8 %copy-start.25 = (bf16[64,8,1,16]{0,3,1,2:T(8,128)(2,1)S(1)}, bf16[64,8,1,16]{0,3,1,2:T(8,128)(2,1)}, u32[]{:S(2)}) copy-start(bf16[64,8,1,16]{0,3,1,2:T(8,128)(2,1)} %get-tuple-element.346) | copy-start | bytes 49156
  27.7 5.8 %copy-start.26 = (bf16[64,8,1,16]{0,3,1,2:T(8,128)(2,1)S(1)}, bf16[64,8,1,16]{0,3,1,2:T(8,128)(2,1)}, u32[]{:S(2)}) copy-start(bf16[64,8,1,16]{0,3,1,2:T(8,128)(2,1)} %get-tuple-element.347) | copy-start | bytes 49156
  32.1 4.7 copy-start.22
  32.1 4.7 copy-start.23
  35.5 4.7 copy-start.21
  36.8 6.7 %copy-start.9 = (f32[64,8,1,16]{0,3,1,2:T(8,128)}, f32[64,8,1,16]{0,3,1,2:T(8,128)S(1)}, u32[]{:S(2)}) copy-start(f32[64,8,1,16]{0,3,1,2:T(8,128)S(1)} %convolution_bitcast_fusion.14) | copy-start | bytes 98308
  40.2 3.4 copy-start.11
  43.5 0.6 copy-start.13
  44.1 3.3 copy-start.5
  50.9 5.7 %copy-start.7 = (bf16[16,8,8,128]{3,2,1,0:T(8,128)(2,1)S(1)}, bf16[16,8,8,128]{3,2,1,0:T(8,128)(2,1)}, u32[]{:S(2)}) copy-start(bf16[16,8,8,128]{3,2,1,0:T(8,128)(2,1)} %param.9) | copy-start | bytes 786436
  53.5 12.9 %collective-permute-start.2 = (bf16[16,1,8,128]{3,0,2,1:T(8,128)(2,1)}, bf16[16,1,8,128]{3,0,2,1:T(8,128)(2,1)}, u32[]{:S(2)}, u32[]{:S(2)}) collective-permute-start(bf16[16,1,8,128]{3,0,2,1:T(8,128)(2,1)} %get-tuple-element.297), channel_id=1, source_target_pairs={{0,8},{8,16},{16,24},{24,32},{32,40},{40,48},{48,56},{56,64},{64,7... | collective-permute-start | bytes 98312 | tf_op jit(solution)/shard_map/ppermute | solution.py:15
  55.4 11.0 %collective-permute-start.3 = (bf16[16,1,8,128]{3,0,2,1:T(8,128)(2,1)}, bf16[16,1,8,128]{3,0,2,1:T(8,128)(2,1)S(1)}, u32[]{:S(2)}, u32[]{:S(2)}) collective-permute-start(bf16[16,1,8,128]{3,0,2,1:T(8,128)(2,1)} %get-tuple-element.298), channel_id=1, source_target_pairs={{8,0},{16,8},{24,16},{32,24},{40,32},{48,40},{56,48},{64,56},{72,6... | collective-permute-start | bytes 98312 | tf_op jit(solution)/shard_map/ppermute | solution.py:18
  67.7 10.6 %collective-permute-start.4 = (bf16[16,10,1,128]{3,0,2,1:T(8,128)(2,1)}, bf16[16,10,1,128]{3,0,2,1:T(8,128)(2,1)}, u32[]{:S(2)}, u32[]{:S(2)}) collective-permute-start(bf16[16,10,1,128]{3,0,2,1:T(8,128)(2,1)} %get-tuple-element.286), channel_id=1, source_target_pairs={{0,1},{1,2},{2,3},{3,4},{4,5},{5,6},{6,7},{8,9},{9,10},{10,11},{11... | collective-permute-start | bytes 122888 | tf_op jit(solution)/shard_map/ppermute | solution.py:15
  71.9 7.7 %collective-permute-start.5 = (bf16[16,10,1,128]{3,0,2,1:T(8,128)(2,1)}, bf16[16,10,1,128]{3,0,2,1:T(8,128)(2,1)}, u32[]{:S(2)}, u32[]{:S(2)}) collective-permute-start(bf16[16,10,1,128]{3,0,2,1:T(8,128)(2,1)} %get-tuple-element.287), channel_id=1, source_target_pairs={{1,0},{2,1},{3,2},{4,3},{5,4},{6,5},{7,6},{9,8},{10,9},{11,10},{12... | collective-permute-start | bytes 122888 | tf_op jit(solution)/shard_map/ppermute | solution.py:18
  84.1 1.0 copy-start.1
  84.1 1.0 copy-start.15
  85.5 4.7 collective-permute-start.6
  90.2 0.6 copy-start.19
  93.9 85.2 %collective-permute-start.7 = (bf16[16,1,8,128]{3,0,2,1:T(8,128)(2,1)S(1)}, bf16[16,1,8,128]{3,0,2,1:T(8,128)(2,1)S(1)}, u32[]{:S(2)}, u32[]{:S(2)}) collective-permute-start(bf16[16,1,8,128]{3,0,2,1:T(8,128)(2,1)S(1)} %slice.2150), channel_id=1, source_target_pairs={{8,0},{16,8},{24,16},{32,24},{40,32},{48,40},{56,48},{64,56},{72,6... | collective-permute-start | bytes 98312 | tf_op jit(solution)/shard_map/ppermute | solution.py:18
  179.2 4.3 copy-start.17
  179.8 10.6 %collective-permute-start.8 = (bf16[16,10,1,128]{3,0,2,1:T(8,128)(2,1)}, bf16[16,10,1,128]{3,0,2,1:T(8,128)(2,1)S(1)}, u32[]{:S(2)}, u32[]{:S(2)}) collective-permute-start(bf16[16,10,1,128]{3,0,2,1:T(8,128)(2,1)} %get-tuple-element.282), channel_id=1, source_target_pairs={{0,1},{1,2},{2,3},{3,4},{4,5},{5,6},{6,7},{8,9},{9,10},{10,11},{11... | collective-permute-start | bytes 122888 | tf_op jit(solution)/shard_map/ppermute | solution.py:15
  183.4 7.6 %collective-permute-start.9 = (bf16[16,10,1,128]{3,0,2,1:T(8,128)(2,1)}, bf16[16,10,1,128]{3,0,2,1:T(8,128)(2,1)S(1)}, u32[]{:S(2)}, u32[]{:S(2)}) collective-permute-start(bf16[16,10,1,128]{3,0,2,1:T(8,128)(2,1)} %get-tuple-element.283), channel_id=1, source_target_pairs={{1,0},{2,1},{3,2},{4,3},{5,4},{6,5},{7,6},{9,8},{10,9},{11,10},{12... | collective-permute-start | bytes 122888 | tf_op jit(solution)/shard_map/ppermute | solution.py:18
  190.4 1.2 copy-start.20
  195.4 0.9 copy-start.18
  197.3 1.0 copy-start.8
  212.6 34.4 %copy-start.10 = (f32[64,8,1,16]{0,3,1,2:T(8,128)S(1)}, f32[64,8,1,16]{0,3,1,2:T(8,128)}, u32[]{:S(2)}) copy-start(f32[64,8,1,16]{0,3,1,2:T(8,128)} %copy-done.9) | copy-start | bytes 98308
  212.6 34.4 %copy-start.12 = (f32[64,8,1,16]{0,3,1,2:T(8,128)S(1)}, f32[64,8,1,16]{0,3,1,2:T(8,128)}, u32[]{:S(2)}) copy-start(f32[64,8,1,16]{0,3,1,2:T(8,128)} %copy-done.11) | copy-start | bytes 98308
  212.6 34.3 %copy-start.14 = (f32[64,8,1,16]{0,3,1,2:T(8,128)S(1)}, f32[64,8,1,16]{0,3,1,2:T(8,128)}, u32[]{:S(2)}) copy-start(f32[64,8,1,16]{0,3,1,2:T(8,128)} %copy-done.13) | copy-start | bytes 98308
  212.6 42.9 %copy-start = (bf16[8,8,8,16,1,1,16]{6,3,2,1,0,5,4:T(8,128)(2,1)S(1)}, bf16[8,8,8,16,1,1,16]{6,3,2,1,0,5,4:T(8,128)(2,1)}, u32[]{:S(2)}) copy-start(bf16[8,8,8,16,1,1,16]{6,3,2,1,0,5,4:T(8,128)(2,1)} %copy.70) | copy-start | bytes 786436
  212.6 42.9 %copy-start.6 = (bf16[64,32,1,16]{0,3,1,2:T(8,128)(2,1)S(1)}, bf16[64,32,1,16]{0,3,1,2:T(8,128)(2,1)}, u32[]{:S(2)}) copy-start(bf16[64,32,1,16]{0,3,1,2:T(8,128)(2,1)} %copy-done.5) | copy-start | bytes 196612
  247.0 12.4 %collective-permute-start.10 = (bf16[64,32,1,16]{0,3,1,2:T(8,128)(2,1)S(1)}, bf16[64,32,1,16]{0,3,1,2:T(8,128)(2,1)S(1)}, u32[]{:S(2)}, u32[]{:S(2)}) collective-permute-start(bf16[64,32,1,16]{0,3,1,2:T(8,128)(2,1)S(1)} %fusion.37), channel_id=1, source_target_pairs={{0,1},{1,2},{2,3},{3,4},{4,5},{5,6},{6,7},{8,9},{9,10},{10,11},{11... | collective-permute-start | bytes 196616 | tf_op jit(solution)/shard_map/ppermute | solution.py:15
  252.9 8.9 %collective-permute-start.11 = (bf16[64,32,1,16]{0,3,1,2:T(8,128)(2,1)S(1)}, bf16[64,32,1,16]{0,3,1,2:T(8,128)(2,1)S(1)}, u32[]{:S(2)}, u32[]{:S(2)}) collective-permute-start(bf16[64,32,1,16]{0,3,1,2:T(8,128)(2,1)S(1)} %fusion.37), channel_id=1, source_target_pairs={{1,0},{2,1},{3,2},{4,3},{5,4},{6,5},{7,6},{9,8},{10,9},{11,10},{12... | collective-permute-start | bytes 196616 | tf_op jit(solution)/shard_map/ppermute | solution.py:18
  255.5 2.8 copy-start.16
Sparse Core Ops, SparseCore 0:
  259.6 268.3 all-reduce.7
where the time goes:
time: 542 us; the launch traced here: 539 us
  waiting for transfers between devices  261 us (48%)
  blocking collectives  118 us (22%)
  local copies, waits for them, and re-layouts  76.8 us (14%)
  starting transfers between devices  41 us (8%)
  matrix products  16.3 us (3%)
  between operations  15.5 us (3%)
  other arithmetic  11.2 us (2%)
    psum x1, waiting for transfers between devices, on_device(): lax.psum((enc_total, dec_total, jnp.einsum('kn,cn->kc', grad_rows, enc_fl...  256 us
    psum x1, blocking collectives, on_device(): lax.psum((enc_total, dec_total, jnp.einsum('kn,cn->kc', grad_rows, enc_fl...  83.9 us
    all_gather x1, blocking collectives, on_device(): enc_grad = lax.all_gather(enc_grad_own, 'wide', axis=1, tiled=True)  33.9 us
    ppermute x6, starting transfers between devices, padded_2(): lax.ppermute(lax.slice_in_dim(block, block.shape[dim] - width, None, axis...  24 us
    ppermute x6, starting transfers between devices, padded_2(): lax.ppermute(lax.slice_in_dim(block, 0, width, axis=dim), axis, backward)  17.1 us
    concatenate x15, local copies, waits for them, and re-layouts, columns(): return jnp.concatenate(pieces, 0)  15.1 us
    unnamed x175, local copies, waits for them, and re-layouts  14.7 us
    slice x17, local copies, waits for them, and re-layouts, columns(): padded[:, first + shift_x:first + shift_x + count, shift_z:shift_z + dept...  11.8 us
  transfers between devices with their start and end apart: 13, of which 4 were waited for; matrix products, arithmetic and copies ran while one was open for 7% of the time, Pallas kernels for 0%

commit v1 on v0

--- a/solution.py
+++ b/solution.py
@@ -156,7 +156,9 @@
         .reshape(chans, own_planes, depth, width)
         .astype(jnp.bfloat16)
     )
-    enc_grad = lax.all_gather(enc_grad_own, "wide", axis=1, tiled=True)
+    enc_grad = jnp.concatenate(
+        lax.all_to_all(jnp.stack([enc_grad_own] * lax.axis_size("wide")), "wide", 0, 0), axis=1
+    )
     enc_pre_grad = (enc_grad.astype(jnp.float32) * silu_slope(enc_pre)).astype(jnp.bfloat16)
     grad_own = lax.dynamic_slice_in_dim(enc_pre_grad, first_plane, own_planes, 1)
     dark_own = lax.dynamic_slice_in_dim(dark_padded, first_plane, own_planes + 2, 1)

time: 542 us -> 522 us (0.963)
  blocking collectives: 118 us -> 83.9 us
  starting transfers between devices: 41 us -> 47.9 us
    all_gather x1 -> x0, blocking collectives: 33.9 us -> none  [on_device(): enc_grad = lax.all_gather(enc_grad_own, 'wide', axis=1, tiled=True)]
    all_to_all x0 -> x1, starting transfers between devices: none -> 6.87 us  [on_device(): lax.all_to_all(jnp.stack([enc_grad_own] * lax.axis_size('wide')), 'wide',...]
    unnamed x175 -> x194, local copies, waits for them, and re-layouts: 14.7 us -> 15.2 us
  transfers between devices with their start and end apart: 13 -> 14, of which waited for: 4 -> 5; matrix products, arithmetic and copies ran while one was open for 7% -> 7% of each run, Pallas kernels for 0% -> 0%
where the time goes in v1:
time: 522 us; the launch traced here: 519 us
  waiting for transfers between devices  266 us (51%)
  blocking collectives  83.9 us (16%)
  local copies, waits for them, and re-layouts  76.8 us (15%)
  starting transfers between devices  47.9 us (9%)
  matrix products  18 us (3%)
  between operations  15.6 us (3%)
  other arithmetic  11.2 us (2%)
    psum x1, waiting for transfers between devices, on_device(): lax.psum((enc_total, dec_total, jnp.einsum('kn,cn->kc', grad_rows, enc_fl...  255 us
    psum x1, blocking collectives, on_device(): lax.psum((enc_total, dec_total, jnp.einsum('kn,cn->kc', grad_rows, enc_fl...  83.9 us
    ppermute x6, starting transfers between devices, padded_2(): lax.ppermute(lax.slice_in_dim(block, block.shape[dim] - width, None, axis...  23.9 us
    ppermute x6, starting transfers between devices, padded_2(): lax.ppermute(lax.slice_in_dim(block, 0, width, axis=dim), axis, backward)  16.8 us
    unnamed x194, local copies, waits for them, and re-layouts  15.2 us
    concatenate x15, local copies, waits for them, and re-layouts, columns(): return jnp.concatenate(pieces, 0)  14.5 us
    slice x17, local copies, waits for them, and re-layouts, columns(): padded[:, first + shift_x:first + shift_x + count, shift_z:shift_z + dept...  12 us
  transfers between devices with their start and end apart: 14, of which 5 were waited for; matrix products, arithmetic and copies ran while one was open for 7% of the time, Pallas kernels for 0%

profile of v1, /device:TPU:2, one launch (start us, length us, event | category | flops | bytes accessed | tf_op | source)
XLA Modules:
  0.0 519.5 jit_solution(11381158895782061075)
XLA Ops:
  7.2 5.1 collective-permute-start
  12.3 3.1 collective-permute-start.1
  15.4 1.6 fusion.88
  17.0 1.3 copy.82
  18.8 3.0 copy.91
  27.7 1.7 fusion.87
  30.1 2.0 concatenate.180
  32.2 1.3 convolution_bitcast_fusion.15
  33.6 2.0 concatenate.182
  35.6 1.3 convolution_bitcast_fusion.14
  37.0 2.0 concatenate.184
  39.0 1.3 convolution_bitcast_fusion.13
  40.4 2.0 concatenate.186
  42.3 1.3 convolution_bitcast_fusion.12
  44.4 2.7 convert_element_type.91
  47.1 3.5 copy.140
  50.6 1.9 copy.93
  53.1 1.9 collective-permute-start.2
  55.0 1.3 collective-permute-start.3
  58.3 1.5 rev.6
  59.9 1.7 copy.99
  61.5 1.7 reshape.381
  63.2 1.7 copy.106
  66.0 1.3 pad_maximum_fusion.13
  67.3 4.2 collective-permute-start.4
  71.5 4.0 collective-permute-start.5
  76.3 1.5 concatenate.219
  77.8 1.4 collective-permute-done.5
  79.2 1.3 fusion.17
  85.2 3.3 collective-permute-start.6
  93.6 1.3 collective-permute-start.7
  94.9 83.9 %psum.23 = f32[16,432]{1,0:T(8,128)S(1)} all-reduce(f32[16,432]{1,0:T(8,128)S(1)} %fusion.7), channel_id=1, replica_groups=mesh['wide'=32,'narrow'=8] {'wide','narrow'}, use_global_device_ids=true, to_apply=%region_2.3 | all-reduce | flops 6912 | bytes 55296 | tf_op jit(solution)/shard_map/psum | solution.py:175
  179.5 3.6 collective-permute-start.8
  183.1 4.6 collective-permute-start.9
  198.1 1.7 copy.107
  199.9 4.1 copy.114
  204.0 3.5 copy.108
  207.5 4.7 reshape.371
  213.4 6.9 %all-to-all-start = ((bf16[32,2,512]{2,1,0:T(2,128)(2,1)}), bf16[32,2,512]{2,1,0:T(2,128)(2,1)S(1)}, u32[]{:S(2)}, u32[]{:S(2)}) async-start(bf16[32,2,512]{2,1,0:T(2,128)(2,1)} %reshape.395), calls=%async_computation | async-start | bytes 131072 | tf_op jit(solution)/shard_map/all_to_all | solution.py:160
  220.6 4.5 fusion.1
  225.1 4.3 all-to-all-done
  229.6 5.8 %collective-permute-start.10 = (bf16[64,32,1,16]{0,3,1,2:T(8,128)(2,1)S(1)}, bf16[64,32,1,16]{0,3,1,2:T(8,128)(2,1)S(1)}, u32[]{:S(2)}, u32[]{:S(2)}) collective-permute-start(bf16[64,32,1,16]{0,3,1,2:T(8,128)(2,1)S(1)} %fusion.37), channel_id=1, source_target_pairs={{0,1},{1,2},{2,3},{3,4},{4,5},{5,6},{6,7},{8,9},{9,10},{10,11},{11... | collective-permute-start | bytes 196616 | tf_op jit(solution)/shard_map/ppermute | solution.py:15
  235.5 2.4 collective-permute-start.11
  239.0 4.8 collective-permute-done.11
  247.3 1.3 concatenate.214
  248.6 1.3 concatenate.215
  253.4 254.9 %all-reduce.8.cloned.1.call-done = (f32[64,1728]{1,0:T(8,128)}, f32[512,16,64]{2,0,1:T(8,128)}) async-done(((f32[64,1728]{1,0:T(8,128)}, f32[512,16,64]{2,0,1:T(8,128)}), (f32[64,1728]{1,0:T(8,128)}, f32[512,16,64]{2,0,1:T(8,128)})) %all-reduce.8.cloned.1.call-update) | async-done | bytes 2539536 | tf_op jit(solution)/shard_map/psum | solution.py:175
  509.8 1.4 copy.117
  (300 shorter events, 44.8 us)
Async XLA Ops:
  7.2 14.7 %collective-permute-start = (bf16[64,32,1,16]{0,3,1,2:T(8,128)(2,1)}, bf16[64,32,1,16]{0,3,1,2:T(8,128)(2,1)S(1)}, u32[]{:S(2)}, u32[]{:S(2)}) collective-permute-start(bf16[64,32,1,16]{0,3,1,2:T(8,128)(2,1)} %bitcast.238), channel_id=1, source_target_pairs={{0,1},{1,2},{2,3},{3,4},{4,5},{5,6},{6,7},{8,9},{9,10},{10,11},{11... | collective-permute-start | bytes 196616 | tf_op jit(solution)/shard_map/ppermute | solution.py:15
  12.3 10.2 %collective-permute-start.1 = (bf16[64,32,1,16]{0,3,1,2:T(8,128)(2,1)}, bf16[64,32,1,16]{0,3,1,2:T(8,128)(2,1)}, u32[]{:S(2)}, u32[]{:S(2)}) collective-permute-start(bf16[64,32,1,16]{0,3,1,2:T(8,128)(2,1)} %bitcast.239), channel_id=1, source_target_pairs={{1,0},{2,1},{3,2},{4,3},{5,4},{6,5},{7,6},{9,8},{10,9},{11,10},{12... | collective-permute-start | bytes 196616 | tf_op jit(solution)/shard_map/ppermute | solution.py:18
  18.8 3.7 copy-start.1
  21.8 0.7 copy-start.2
  25.3 4.1 copy-start.3
  27.7 5.8 %copy-start.27 = (bf16[64,8,1,16]{0,3,1,2:T(8,128)(2,1)S(1)}, bf16[64,8,1,16]{0,3,1,2:T(8,128)(2,1)}, u32[]{:S(2)}) copy-start(bf16[64,8,1,16]{0,3,1,2:T(8,128)(2,1)} %get-tuple-element.349) | copy-start | bytes 49156
  27.7 5.8 %copy-start.28 = (bf16[64,8,1,16]{0,3,1,2:T(8,128)(2,1)S(1)}, bf16[64,8,1,16]{0,3,1,2:T(8,128)(2,1)}, u32[]{:S(2)}) copy-start(bf16[64,8,1,16]{0,3,1,2:T(8,128)(2,1)} %get-tuple-element.350) | copy-start | bytes 49156
  27.7 5.8 %copy-start.29 = (bf16[64,8,1,16]{0,3,1,2:T(8,128)(2,1)S(1)}, bf16[64,8,1,16]{0,3,1,2:T(8,128)(2,1)}, u32[]{:S(2)}) copy-start(bf16[64,8,1,16]{0,3,1,2:T(8,128)(2,1)} %get-tuple-element.351) | copy-start | bytes 49156
  30.1 3.4 copy-start.30
  30.1 3.4 copy-start.31
  30.1 3.4 copy-start.32
  30.1 3.4 copy-start.33
  32.2 4.8 copy-start.25
  32.2 4.8 copy-start.26
  35.6 4.7 copy-start.20
  35.6 4.7 copy-start.21
  35.6 4.7 copy-start.22
  35.6 4.7 copy-start.23
  35.6 4.7 copy-start.24
  36.9 6.7 %copy-start.8 = (f32[64,8,1,16]{0,3,1,2:T(8,128)}, f32[64,8,1,16]{0,3,1,2:T(8,128)S(1)}, u32[]{:S(2)}) copy-start(f32[64,8,1,16]{0,3,1,2:T(8,128)S(1)} %convolution_bitcast_fusion.14) | copy-start | bytes 98308
  40.3 4.1 copy-start.10
  43.6 3.4 copy-start.12
  43.7 3.3 copy-start.4
  50.6 5.7 %copy-start.6 = (bf16[16,8,8,128]{3,2,1,0:T(8,128)(2,1)S(1)}, bf16[16,8,8,128]{3,2,1,0:T(8,128)(2,1)}, u32[]{:S(2)}) copy-start(bf16[16,8,8,128]{3,2,1,0:T(8,128)(2,1)} %param.9) | copy-start | bytes 786436
  53.1 12.9 %collective-permute-start.2 = (bf16[16,1,8,128]{3,0,2,1:T(8,128)(2,1)}, bf16[16,1,8,128]{3,0,2,1:T(8,128)(2,1)}, u32[]{:S(2)}, u32[]{:S(2)}) collective-permute-start(bf16[16,1,8,128]{3,0,2,1:T(8,128)(2,1)} %get-tuple-element.301), channel_id=1, source_target_pairs={{0,8},{8,16},{16,24},{24,32},{32,40},{40,48},{48,56},{56,64},{64,7... | collective-permute-start | bytes 98312 | tf_op jit(solution)/shard_map/ppermute | solution.py:15
  55.0 11.0 %collective-permute-start.3 = (bf16[16,1,8,128]{3,0,2,1:T(8,128)(2,1)}, bf16[16,1,8,128]{3,0,2,1:T(8,128)(2,1)S(1)}, u32[]{:S(2)}, u32[]{:S(2)}) collective-permute-start(bf16[16,1,8,128]{3,0,2,1:T(8,128)(2,1)} %get-tuple-element.302), channel_id=1, source_target_pairs={{8,0},{16,8},{24,16},{32,24},{40,32},{48,40},{56,48},{64,56},{72,6... | collective-permute-start | bytes 98312 | tf_op jit(solution)/shard_map/ppermute | solution.py:18
  67.3 10.5 %collective-permute-start.4 = (bf16[16,10,1,128]{3,0,2,1:T(8,128)(2,1)}, bf16[16,10,1,128]{3,0,2,1:T(8,128)(2,1)}, u32[]{:S(2)}, u32[]{:S(2)}) collective-permute-start(bf16[16,10,1,128]{3,0,2,1:T(8,128)(2,1)} %get-tuple-element.290), channel_id=1, source_target_pairs={{0,1},{1,2},{2,3},{3,4},{4,5},{5,6},{6,7},{8,9},{9,10},{10,11},{11... | collective-permute-start | bytes 122888 | tf_op jit(solution)/shard_map/ppermute | solution.py:15
  71.5 7.7 %collective-permute-start.5 = (bf16[16,10,1,128]{3,0,2,1:T(8,128)(2,1)}, bf16[16,10,1,128]{3,0,2,1:T(8,128)(2,1)}, u32[]{:S(2)}, u32[]{:S(2)}) collective-permute-start(bf16[16,10,1,128]{3,0,2,1:T(8,128)(2,1)} %get-tuple-element.291), channel_id=1, source_target_pairs={{1,0},{2,1},{3,2},{4,3},{5,4},{6,5},{7,6},{9,8},{10,9},{11,10},{12... | collective-permute-start | bytes 122888 | tf_op jit(solution)/shard_map/ppermute | solution.py:18
  83.8 1.0 copy-start
  83.8 1.0 copy-start.14
  85.2 4.7 collective-permute-start.6
  93.6 85.2 %collective-permute-start.7 = (bf16[16,1,8,128]{3,0,2,1:T(8,128)(2,1)S(1)}, bf16[16,1,8,128]{3,0,2,1:T(8,128)(2,1)S(1)}, u32[]{:S(2)}, u32[]{:S(2)}) collective-permute-start(bf16[16,1,8,128]{3,0,2,1:T(8,128)(2,1)S(1)} %slice.2150), channel_id=1, source_target_pairs={{8,0},{16,8},{24,16},{32,24},{40,32},{48,40},{56,48},{64,56},{72,6... | collective-permute-start | bytes 98312 | tf_op jit(solution)/shard_map/ppermute | solution.py:18
  178.8 4.3 copy-start.16
  179.5 10.6 %collective-permute-start.8 = (bf16[16,10,1,128]{3,0,2,1:T(8,128)(2,1)}, bf16[16,10,1,128]{3,0,2,1:T(8,128)(2,1)S(1)}, u32[]{:S(2)}, u32[]{:S(2)}) collective-permute-start(bf16[16,10,1,128]{3,0,2,1:T(8,128)(2,1)} %get-tuple-element.286), channel_id=1, source_target_pairs={{0,1},{1,2},{2,3},{3,4},{4,5},{5,6},{6,7},{8,9},{9,10},{10,11},{11... | collective-permute-start | bytes 122888 | tf_op jit(solution)/shard_map/ppermute | solution.py:15
  183.1 7.6 %collective-permute-start.9 = (bf16[16,10,1,128]{3,0,2,1:T(8,128)(2,1)}, bf16[16,10,1,128]{3,0,2,1:T(8,128)(2,1)S(1)}, u32[]{:S(2)}, u32[]{:S(2)}) collective-permute-start(bf16[16,10,1,128]{3,0,2,1:T(8,128)(2,1)} %get-tuple-element.287), channel_id=1, source_target_pairs={{1,0},{2,1},{3,2},{4,3},{5,4},{6,5},{7,6},{9,8},{10,9},{11,10},{12... | collective-permute-start | bytes 122888 | tf_op jit(solution)/shard_map/ppermute | solution.py:18
  190.1 1.2 copy-start.19
  195.1 0.9 copy-start.17
  197.0 1.0 copy-start.7
  212.2 8.4 %copy-start.5 = (bf16[64,32,1,16]{0,3,1,2:T(8,128)(2,1)S(1)}, bf16[64,32,1,16]{0,3,1,2:T(8,128)(2,1)}, u32[]{:S(2)}) copy-start(bf16[64,32,1,16]{0,3,1,2:T(8,128)(2,1)} %copy-done.4) | copy-start | bytes 196612
  213.4 15.9 %all-to-all-start = ((bf16[32,2,512]{2,1,0:T(2,128)(2,1)}), bf16[32,2,512]{2,1,0:T(2,128)(2,1)S(1)}, u32[]{:S(2)}, u32[]{:S(2)}) async-start(bf16[32,2,512]{2,1,0:T(2,128)(2,1)} %reshape.395), calls=%async_computation | async-start | bytes 131072 | tf_op jit(solution)/shard_map/all_to_all | solution.py:160
  220.3 288.0 %all-reduce.8.cloned.1.call-start = ((), (), s32[]{:S(2)}) async-start(), calls=%async_computation.1 | async-start | bytes 9306112 | tf_op jit(solution)/shard_map/psum | solution.py:175
  220.6 8.9 %copy-start.9 = (f32[64,8,1,16]{0,3,1,2:T(8,128)S(1)}, f32[64,8,1,16]{0,3,1,2:T(8,128)}, u32[]{:S(2)}) copy-start(f32[64,8,1,16]{0,3,1,2:T(8,128)} %copy-done.8) | copy-start | bytes 98308
  220.6 8.9 %copy-start.11 = (f32[64,8,1,16]{0,3,1,2:T(8,128)S(1)}, f32[64,8,1,16]{0,3,1,2:T(8,128)}, u32[]{:S(2)}) copy-start(f32[64,8,1,16]{0,3,1,2:T(8,128)} %copy-done.10) | copy-start | bytes 98308
  220.6 8.9 %copy-start.13 = (f32[64,8,1,16]{0,3,1,2:T(8,128)S(1)}, f32[64,8,1,16]{0,3,1,2:T(8,128)}, u32[]{:S(2)}) copy-start(f32[64,8,1,16]{0,3,1,2:T(8,128)} %copy-done.12) | copy-start | bytes 98308
  220.6 17.3 %copy-start.15 = (bf16[1728,1,1,16]{0,3,1,2:T(8,128)(2,1)S(1)}, bf16[1728,1,1,16]{0,3,1,2:T(8,128)(2,1)}, u32[]{:S(2)}) copy-start(bf16[1728,1,1,16]{0,3,1,2:T(8,128)(2,1)} %concatenate.219) | copy-start | bytes 165892
  229.6 9.4 %collective-permute-start.10 = (bf16[64,32,1,16]{0,3,1,2:T(8,128)(2,1)S(1)}, bf16[64,32,1,16]{0,3,1,2:T(8,128)(2,1)S(1)}, u32[]{:S(2)}, u32[]{:S(2)}) collective-permute-start(bf16[64,32,1,16]{0,3,1,2:T(8,128)(2,1)S(1)} %fusion.37), channel_id=1, source_target_pairs={{0,1},{1,2},{2,3},{3,4},{4,5},{5,6},{6,7},{8,9},{9,10},{10,11},{11... | collective-permute-start | bytes 196616 | tf_op jit(solution)/shard_map/ppermute | solution.py:15
  235.5 8.4 %collective-permute-start.11 = (bf16[64,32,1,16]{0,3,1,2:T(8,128)(2,1)S(1)}, bf16[64,32,1,16]{0,3,1,2:T(8,128)(2,1)S(1)}, u32[]{:S(2)}, u32[]{:S(2)}) collective-permute-start(bf16[64,32,1,16]{0,3,1,2:T(8,128)(2,1)S(1)} %fusion.37), channel_id=1, source_target_pairs={{1,0},{2,1},{3,2},{4,3},{5,4},{6,5},{7,6},{9,8},{10,9},{11,10},{12... | collective-permute-start | bytes 196616 | tf_op jit(solution)/shard_map/ppermute | solution.py:18
  245.0 2.3 copy-start.34
  (1 other events, 0.6 us)
Sparse Core Ops, SparseCore 0:
  239.1 269.1 all-reduce.7
